TPU v7x, 32 devices: a whole 2x2x4 slice. The times are simulated.
32 devices in a mesh: dp: 8 (over y, x, core), mp: 4 (over z).
Axes of the slice: x: 2, y: 2, z: 4, core: 2. Of those that a mesh axis runs over, the one named last changes fastest.
Arguments:
- tokens: bfloat16 [32768, 512], P(('dp', 'mp')), may hold values from -6 to 6
- qkv_weight: bfloat16 [512, 1536], replicated, may hold values from -0.25 to 0.25
- out_weight: bfloat16 [512, 512], replicated, may hold values from -2 to 2
- norm1_gain: float32 [512], replicated, may hold values from 0.1 to 1.9
- norm1_shift: float32 [512], replicated, may hold values from -3 to 3
- norm2_gain: float32 [512], replicated, may hold values from 0.1 to 1.9
- norm2_shift: float32 [512], replicated, may hold values from -3 to 3
- up_weight: bfloat16 [512, 2048], P(None, 'mp'), may hold values from -0.25 to 0.25
- up_bias: bfloat16 [2048], P('mp'), may hold values from -3 to 3
- down_weight: bfloat16 [2048, 512], P('mp'), may hold values from -0.125 to 0.125
- down_bias: float32 [512], replicated, may hold values from -3 to 3
- lengths: int32 [17], replicated, may hold values from 512 to 16384, as said below
- cotangent: bfloat16 [32768, 512], P(('dp', 'mp')), may hold values from -6 to 6
Outputs:
- output: bfloat16 [32768, 512], P(('dp', 'mp'))
- input_grad: bfloat16 [32768, 512], P(('dp', 'mp'))
- qkv_grad: float32 [512, 1536], replicated
- out_grad: float32 [512, 512], replicated
- norm1_gain_grad: float32 [512], replicated
- norm1_shift_grad: float32 [512], replicated
- norm2_gain_grad: float32 [512], replicated
- norm2_shift_grad: float32 [512], replicated
- up_grad: float32 [512, 2048], P(None, 'mp')
- up_bias_grad: float32 [2048], P('mp')
- down_grad: float32 [2048, 512], P('mp')
- down_bias_grad: float32 [512], replicated
Inputs may be any that keep to these rules, and one draw needn't show every extreme that they name: The 17 lengths add up to 32768; 1 of them equal 16384, and the others lie between 512 and 1536, both ends reached.
All inputs are finite; a program needn't handle non-finite values.
Results may differ from a plain program's by a relative error of at most 0.012.
Values may be sent and summed in bfloat16 or wider, within the bound.
No kernel may reach another device: no remote copies, remote signals or barrier semaphores. Data moves between devices by JAX's collectives and lax.ppermute only.
A program may use at most 192 MiB of HBM per device.

v0:
```python
import jax
import jax.numpy as jnp
from jax import lax
from jax.sharding import PartitionSpec as P

HEADS = 8
HEAD_DIM = 64
BLK = 512
NORM_EPS = 1e-05
SCORE_EPS = 1e-06
EXACT_MODE = lax.Precision.HIGHEST


def carried_in(array, axis, combine, identity):
    peers, position = (lax.axis_size(axis), lax.axis_index(axis))
    everything = jax.tree.map(
        lambda part, kind: lax.all_gather(part.astype(kind), axis),
        array,
        (jnp.bfloat16, jnp.bfloat16, jnp.bfloat16),
    )
    start = jax.tree.map(
        lambda part, zero: jnp.broadcast_to(jnp.asarray(zero, part.dtype), part.shape),
        array,
        identity,
    )

    def lap(k, before):
        reached = k < position
        new = combine(
            before, jax.tree.map(lambda part, own: part[k].astype(own.dtype), everything, array)
        )
        return jax.tree.map(lambda a, b: jnp.where(reached, a, b), new, before)

    return lax.fori_loop(0, peers, lap, start)


def carried_in_2(array, axis, join, neutral):
    count = lax.axis_size(axis)
    place = lax.axis_index(axis)
    ahead = count - 1 - place
    gathered = jax.tree.map(
        lambda a, kind: lax.all_gather(a.astype(kind), axis),
        array,
        jax.tree.map(lambda a: jnp.bfloat16 if a.dtype == jnp.float32 else a.dtype, array),
    )
    state = jax.tree.map(lambda a, e: jnp.zeros_like(a) + jnp.asarray(e, a.dtype), array, neutral)

    def one(lap, state):
        source = count - 1 - lap
        return join(
            state,
            jax.tree.map(
                lambda a, own: lax.dynamic_index_in_dim(a, source, 0, False).astype(own.dtype),
                gathered,
                array,
            ),
        )

    return lax.fori_loop(0, ahead, one, state)


def normalize(rows, gain, shift):
    centred = rows - jnp.mean(rows, axis=-1, keepdims=True)
    inv_std = lax.rsqrt(jnp.mean(centred * centred, axis=-1, keepdims=True) + NORM_EPS)
    scaled = centred * inv_std
    return (scaled * gain + shift, scaled, inv_std)


def normalize_back(upstream, scaled, inv_std, gain):
    weighted = upstream * gain
    centred = weighted - jnp.mean(weighted, axis=-1, keepdims=True)
    inner = centred - scaled * jnp.mean(weighted * scaled, axis=-1, keepdims=True)
    return (inner * inv_std, jnp.sum(upstream * scaled, axis=0), jnp.sum(upstream, axis=0))


def feature_map(values):
    return jax.nn.elu(values) + 1.0


def feature_slope(values):
    return jnp.where(values > 0, 1.0, jnp.exp(jnp.minimum(values, 0.0)))


def gelu_slope(values):
    return (
        0.5 * (1.0 + lax.erf(values * 0.7071067811865476))
        + values * jnp.exp(-0.5 * values * values) * 0.3989422804014327
    )


def segment_rows(lengths, first, count):
    ends = jnp.cumsum(lengths)
    starts = ends - lengths
    places = first + jnp.arange(count, dtype=jnp.int32)
    segment = jnp.sum((ends[None, :] <= places[:, None]).astype(jnp.int32), axis=1)
    opening = jnp.sum((starts[None, :] == places[:, None]).astype(jnp.int32), axis=1)
    return (segment, opening)


def block_masks(segment, opening, start):
    block_seg = lax.dynamic_slice_in_dim(segment, start, BLK)
    first_open = lax.dynamic_slice_in_dim(opening, start, 1)[0]
    carried = ((block_seg == block_seg[0]) & (first_open == 0)).astype(jnp.float32)
    ending = (block_seg == block_seg[-1]).astype(jnp.float32)
    places = jnp.arange(BLK)
    allowed = (
        (places[None, :] <= places[:, None]) & (block_seg[None, :] == block_seg[:, None])
    ).astype(jnp.float32)
    return (carried, ending, allowed)


def join_states(earlier, later):
    keep = 1.0 - later[2]
    return (
        later[0] + keep * earlier[0],
        later[1] + keep * earlier[1],
        jnp.maximum(earlier[2], later[2]),
    )


def local(
    tokens,
    qkv_weight,
    out_weight,
    norm1_gain,
    norm1_shift,
    norm2_gain,
    norm2_shift,
    up_weight,
    up_bias,
    down_weight,
    down_bias,
    lengths,
    cotangent,
):
    rows = tokens.shape[0]
    width = tokens.shape[1]
    span = rows * lax.axis_size("mp")
    blocks = span // BLK
    group_first = lax.axis_index("dp") * span
    own_start = lax.axis_index("mp") * rows
    segment, opening = segment_rows(lengths, group_first, span)
    continuing = ((segment == segment[0]) & (opening[0] == 0)).astype(jnp.float32)
    reset = 1.0 - continuing[-1]
    inputs = tokens.astype(jnp.float32)
    normed_one, scaled_one, inv_one = normalize(inputs, norm1_gain, norm1_shift)
    normed_low = normed_one.astype(jnp.bfloat16)
    group_rows = lax.all_gather(normed_low, "mp", axis=0, tiled=True)

    def features(start):
        rows_in = lax.dynamic_slice_in_dim(group_rows, start, BLK)
        projected = jnp.dot(rows_in, qkv_weight, preferred_element_type=jnp.float32)
        query = projected[:, :width].reshape(BLK, HEADS, HEAD_DIM)
        keys = projected[:, width : 2 * width].reshape(BLK, HEADS, HEAD_DIM)
        values = projected[:, 2 * width :].reshape(BLK, HEADS, HEAD_DIM)
        return (query, keys, values)

    def forward_block(carry, index):
        state, total = carry
        start = index * BLK
        query, keys, values = features(start)
        query_low = feature_map(query).astype(jnp.bfloat16)
        key_low = feature_map(keys).astype(jnp.bfloat16)
        value_low = values.astype(jnp.bfloat16)
        carried, ending, allowed = block_masks(segment, opening, start)
        scores = (
            jnp.einsum("ihd,jhd->hij", query_low, key_low, preferred_element_type=jnp.float32)
            * allowed[None]
        )
        query_wide = query_low.astype(jnp.float32)
        numerator = jnp.einsum(
            "hij,jhd->ihd",
            scores.astype(jnp.bfloat16),
            value_low,
            preferred_element_type=jnp.float32,
        )
        numerator = numerator + carried[:, None, None] * jnp.einsum(
            "ihd,hde->ihe", query_wide, state, precision=EXACT_MODE
        )
        denominator = (
            jnp.sum(scores, axis=-1).T
            + carried[:, None] * jnp.einsum("ihd,hd->ih", query_wide, total, precision=EXACT_MODE)
            + SCORE_EPS
        )
        keep = carried[-1]
        key_end = key_low * ending.astype(jnp.bfloat16)[:, None, None]
        new_state = keep * state + jnp.einsum(
            "jhd,jhe->hde", key_end, value_low, preferred_element_type=jnp.float32
        )
        new_total = keep * total + jnp.sum(key_end.astype(jnp.float32), axis=0)
        return ((new_state, new_total), (numerator, denominator, query_low, state, total))

    zero_state = jnp.zeros((HEADS, HEAD_DIM, HEAD_DIM), jnp.float32)
    zero_total = jnp.zeros((HEADS, HEAD_DIM), jnp.float32)
    nothing = jnp.zeros((), jnp.float32)
    (state_end, total_end), kept = lax.scan(
        forward_block, (zero_state, zero_total), jnp.arange(blocks, dtype=jnp.int32)
    )
    numerator = kept[0].reshape(span, HEADS, HEAD_DIM)
    denominator = kept[1].reshape(span, HEADS)
    query_all = kept[2].reshape(span, HEADS, HEAD_DIM)
    block_states = kept[3]
    block_totals = kept[4]
    state_in, total_in, _ = carried_in(
        (state_end, total_end, reset), "dp", join_states, (zero_state, zero_total, nothing)
    )
    query_wide = query_all.astype(jnp.float32)
    numerator = numerator + continuing[:, None, None] * jnp.einsum(
        "ihd,hde->ihe", query_wide, state_in, precision=EXACT_MODE
    )
    denominator = denominator + continuing[:, None] * jnp.einsum(
        "ihd,hd->ih", query_wide, total_in, precision=EXACT_MODE
    )
    context = numerator / denominator[:, :, None]
    context_low = lax.dynamic_slice_in_dim(context.reshape(span, width), own_start, rows).astype(
        jnp.bfloat16
    )
    attended = jnp.dot(context_low, out_weight, preferred_element_type=jnp.float32)
    residual = inputs + attended
    normed_two, scaled_two, inv_two = normalize(residual, norm2_gain, norm2_shift)
    second_low = normed_two.astype(jnp.bfloat16)
    cotangent_wide = cotangent.astype(jnp.float32)
    group_second = lax.all_gather(second_low, "mp", axis=0, tiled=True)
    hidden_in = jnp.dot(group_second, up_weight, preferred_element_type=jnp.float32) + up_bias
    hidden_low = jax.nn.gelu(hidden_in, approximate=False).astype(jnp.bfloat16)
    ffn_out = lax.psum_scatter(
        jnp.dot(hidden_low, down_weight, preferred_element_type=jnp.float32).astype(jnp.bfloat16),
        "mp",
        scatter_dimension=0,
        tiled=True,
    ).astype(jnp.float32)
    group_cotangent = lax.all_gather(cotangent, "mp", axis=0, tiled=True)
    grad_down = jnp.einsum(
        "tf,td->fd", hidden_low, group_cotangent, preferred_element_type=jnp.float32
    )
    grad_hidden = jnp.einsum(
        "td,fd->tf", group_cotangent, down_weight, preferred_element_type=jnp.float32
    )
    hidden_grad = (grad_hidden * gelu_slope(hidden_in)).astype(jnp.bfloat16)
    grad_up_bias = jnp.sum(hidden_grad.astype(jnp.float32), axis=0)
    grad_up = jnp.einsum("td,tf->df", group_second, hidden_grad, preferred_element_type=jnp.float32)
    grad_second = lax.psum_scatter(
        jnp.einsum("tf,df->td", hidden_grad, up_weight, preferred_element_type=jnp.float32).astype(
            jnp.bfloat16
        ),
        "mp",
        scatter_dimension=0,
        tiled=True,
    ).astype(jnp.float32)
    grad_up, grad_up_bias, grad_down = lax.psum((grad_up, grad_up_bias, grad_down), "dp")
    output = (residual + ffn_out + down_bias).astype(jnp.bfloat16)
    grad_second_in, grad_gain_two, grad_shift_two = normalize_back(
        grad_second, scaled_two, inv_two, norm2_gain
    )
    grad_residual = cotangent_wide + grad_second_in
    grad_attended = grad_residual.astype(jnp.bfloat16)
    grad_out = jnp.einsum(
        "ti,to->io", context_low, grad_attended, preferred_element_type=jnp.float32
    )
    grad_context_own = jnp.einsum(
        "to,io->ti", grad_attended, out_weight, preferred_element_type=jnp.float32
    ).astype(jnp.bfloat16)
    grad_context = (
        lax.all_gather(grad_context_own, "mp", axis=0, tiled=True)
        .astype(jnp.float32)
        .reshape(span, HEADS, HEAD_DIM)
    )
    grad_numer = (grad_context / denominator[:, :, None]).astype(jnp.bfloat16)
    grad_denom = -jnp.sum(grad_context * context, axis=-1) / denominator
    local_state = jnp.einsum(
        "ihd,ihe->hde",
        query_all * continuing.astype(jnp.bfloat16)[:, None, None],
        grad_numer,
        preferred_element_type=jnp.float32,
    )
    local_total = jnp.einsum(
        "ih,ihd->hd", continuing[:, None] * grad_denom, query_wide, precision=EXACT_MODE
    )
    state_back, total_back, _ = carried_in_2(
        (local_state, local_total, reset), "dp", join_states, (zero_state, zero_total, nothing)
    )
    prior = jnp.concatenate([jnp.ones((1,), jnp.float32), continuing[BLK - 1 :: BLK][:-1]])
    true_states = block_states + prior[:, None, None, None] * state_in[None]
    true_totals = block_totals + prior[:, None, None] * total_in[None]

    def back_block(carry, index):
        state_grad, total_grad = carry
        start = index * BLK
        query, keys, values = features(start)
        query_low = feature_map(query).astype(jnp.bfloat16)
        key_low = feature_map(keys).astype(jnp.bfloat16)
        value_low = values.astype(jnp.bfloat16)
        carried, ending, allowed = block_masks(segment, opening, start)
        state = true_states[index]
        total = true_totals[index]
        numer_grad = lax.dynamic_slice_in_dim(grad_numer, start, BLK)
        denom_grad = lax.dynamic_slice_in_dim(grad_denom, start, BLK)
        scores = (
            jnp.einsum("ihd,jhd->hij", query_low, key_low, preferred_element_type=jnp.float32)
            * allowed[None]
        )
        weights = scores.astype(jnp.bfloat16)
        weight_grad = (
            jnp.einsum("ihe,jhe->hij", numer_grad, value_low, preferred_element_type=jnp.float32)
            + denom_grad.T[:, :, None]
        )
        score_grad = weight_grad.astype(jnp.bfloat16) * allowed.astype(jnp.bfloat16)[None]
        query_wide_blk = query_low.astype(jnp.float32)
        numer_wide = numer_grad.astype(jnp.float32)
        query_grad = jnp.einsum(
            "hij,jhd->ihd", score_grad, key_low, preferred_element_type=jnp.float32
        )
        query_grad = query_grad + carried[:, None, None] * (
            jnp.einsum("ihe,hde->ihd", numer_wide, state, precision=EXACT_MODE)
            + denom_grad[:, :, None] * total[None]
        )
        key_grad = jnp.einsum(
            "hij,ihd->jhd", score_grad, query_low, preferred_element_type=jnp.float32
        )
        key_grad = key_grad + ending[:, None, None] * (
            jnp.einsum(
                "jhe,hde->jhd", value_low.astype(jnp.float32), state_grad, precision=EXACT_MODE
            )
            + total_grad[None]
        )
        value_grad = jnp.einsum(
            "hij,ihd->jhd", weights, numer_grad, preferred_element_type=jnp.float32
        )
        value_grad = value_grad + ending[:, None, None] * jnp.einsum(
            "jhd,hde->jhe", key_low.astype(jnp.float32), state_grad, precision=EXACT_MODE
        )
        keep = carried[-1]
        prev_state = keep * state_grad + jnp.einsum(
            "ihd,ihe->hde",
            query_low * carried.astype(jnp.bfloat16)[:, None, None],
            numer_grad,
            preferred_element_type=jnp.float32,
        )
        prev_total = keep * total_grad + jnp.einsum(
            "ih,ihd->hd", carried[:, None] * denom_grad, query_wide_blk, precision=EXACT_MODE
        )
        joined = jnp.concatenate(
            [
                (query_grad * feature_slope(query)).reshape(BLK, width),
                (key_grad * feature_slope(keys)).reshape(BLK, width),
                value_grad.reshape(BLK, width),
            ],
            axis=1,
        )
        return ((prev_state, prev_total), joined.astype(jnp.bfloat16))

    _, grad_blocks = lax.scan(
        back_block, (state_back, total_back), jnp.arange(blocks, dtype=jnp.int32), reverse=True
    )
    grad_projected = lax.dynamic_slice_in_dim(grad_blocks.reshape(span, 3 * width), own_start, rows)
    grad_qkv = jnp.einsum(
        "td,tk->dk", normed_low, grad_projected, preferred_element_type=jnp.float32
    )
    grad_first = jnp.einsum(
        "tk,dk->td", grad_projected, qkv_weight, preferred_element_type=jnp.float32
    )
    grad_first_in, grad_gain_one, grad_shift_one = normalize_back(
        grad_first, scaled_one, inv_one, norm1_gain
    )
    input_grad = (grad_residual + grad_first_in).astype(jnp.bfloat16)
    grad_down_bias = jnp.sum(cotangent_wide, axis=0)
    summed = lax.psum(
        (
            grad_qkv,
            grad_out,
            grad_gain_one,
            grad_shift_one,
            grad_gain_two,
            grad_shift_two,
            grad_down_bias,
        ),
        ("dp", "mp"),
    )
    return (
        output,
        input_grad,
        summed[0],
        summed[1],
        summed[2],
        summed[3],
        summed[4],
        summed[5],
        grad_up,
        grad_up_bias,
        grad_down,
        summed[6],
    )


def solution(mesh):
    in_specs = (
        P(("dp", "mp"), None),
        P(),
        P(),
        P(),
        P(),
        P(),
        P(),
        P(None, "mp"),
        P("mp"),
        P("mp", None),
        P(),
        P(),
        P(("dp", "mp"), None),
    )
    out_specs = (
        P(("dp", "mp"), None),
        P(("dp", "mp"), None),
        P(),
        P(),
        P(),
        P(),
        P(),
        P(),
        P(None, "mp"),
        P("mp"),
        P("mp", None),
        P(),
    )
    return jax.shard_map(local, mesh=mesh, in_specs=in_specs, out_specs=out_specs, check_vma=False)
```

profile of v0, /device:TPU:0, one launch (start us, length us, event | category | flops | bytes accessed | tf_op | source)
XLA Modules:
  0.0 1671.2 jit_solution(14207868749321259398)
XLA Ops:
  17.8 15.2 all-reduce
  33.1 62.3 %all-gather.9.cloned.1.call-done = bf16[4096,512]{0,1:T(8,128)(2,1)} async-done(((bf16[1024,512]{0,1:T(8,128)(2,1)}), bf16[4096,512]{0,1:T(8,128)(2,1)}) %all-gather.9.cloned.1.call-update) | async-done | bytes 4194320 | tf_op jit(solution)/shard_map/all_gather | solution.py:148
  95.4 6.5 copy.151
  101.9 482.7 %while.75 = (s32[]{:T(128)}, f32[8,64,64]{2,1,0:T(8,128)S(1)}, f32[8,64]{1,0:T(8,128)S(1)}, f32[8,512,8,64]{1,0,3,2:T(8,128)}, f32[8,512,8]{1,2,0:T(8,128)}, /*i...) while((s32[]{:T(128)}, f32[8,64,64]{2,1,0:T(8,128)S(1)}, ...), condition=%wide.region_8.9_spmd.clone, body=%wide.region_5.8_spmd.clone.sunk | while | flops 1599254528 | bytes 64349520 | solution.py:196
  115.6 5.8 multiply_reduce_fusion.5
  127.1 4.8 fusion.300
  133.0 21.8 %dynamic_update_slice.51 = f32[8,512,8,64]{1,0,3,2:T(8,128)} dynamic-update-slice(f32[8,512,8,64]{1,0,3,2:T(8,128)} %get-tuple-element.1293, f32[1,512,8,64]{1,0,3,2:T(1,128)S(1)} %copy.224, s32[]{:T(128)} %get-tuple-element.1290, s32[]{:T(128)} %constant.253.clone.1..sunk.2, s32[]{:T(128)} %constant.253.clone.1..sunk.2, s32[]{:T(128)} %constant.253.clone.1..sunk.2) | dynamic-update-slice | bytes 2097156 | tf_op jit(solution)/shard_map/while/body/jit(dynamic_update_index_in_dim)/dynamic_update_slice | solution.py:196
  176.0 5.8 multiply_reduce_fusion.5
  187.5 4.8 fusion.300
  193.4 21.8 %dynamic_update_slice.51 = f32[8,512,8,64]{1,0,3,2:T(8,128)} dynamic-update-slice(f32[8,512,8,64]{1,0,3,2:T(8,128)} %get-tuple-element.1293, f32[1,512,8,64]{1,0,3,2:T(1,128)S(1)} %copy.224, s32[]{:T(128)} %get-tuple-element.1290, s32[]{:T(128)} %constant.253.clone.1..sunk.2, s32[]{:T(128)} %constant.253.clone.1..sunk.2, s32[]{:T(128)} %constant.253.clone.1..sunk.2) | dynamic-update-slice | bytes 2097156 | tf_op jit(solution)/shard_map/while/body/jit(dynamic_update_index_in_dim)/dynamic_update_slice | solution.py:196
  236.4 5.8 multiply_reduce_fusion.5
  247.9 4.8 fusion.300
  253.7 21.8 %dynamic_update_slice.51 = f32[8,512,8,64]{1,0,3,2:T(8,128)} dynamic-update-slice(f32[8,512,8,64]{1,0,3,2:T(8,128)} %get-tuple-element.1293, f32[1,512,8,64]{1,0,3,2:T(1,128)S(1)} %copy.224, s32[]{:T(128)} %get-tuple-element.1290, s32[]{:T(128)} %constant.253.clone.1..sunk.2, s32[]{:T(128)} %constant.253.clone.1..sunk.2, s32[]{:T(128)} %constant.253.clone.1..sunk.2) | dynamic-update-slice | bytes 2097156 | tf_op jit(solution)/shard_map/while/body/jit(dynamic_update_index_in_dim)/dynamic_update_slice | solution.py:196
  296.7 5.8 multiply_reduce_fusion.5
  308.2 4.8 fusion.300
  314.0 21.8 %dynamic_update_slice.51 = f32[8,512,8,64]{1,0,3,2:T(8,128)} dynamic-update-slice(f32[8,512,8,64]{1,0,3,2:T(8,128)} %get-tuple-element.1293, f32[1,512,8,64]{1,0,3,2:T(1,128)S(1)} %copy.224, s32[]{:T(128)} %get-tuple-element.1290, s32[]{:T(128)} %constant.253.clone.1..sunk.2, s32[]{:T(128)} %constant.253.clone.1..sunk.2, s32[]{:T(128)} %constant.253.clone.1..sunk.2) | dynamic-update-slice | bytes 2097156 | tf_op jit(solution)/shard_map/while/body/jit(dynamic_update_index_in_dim)/dynamic_update_slice | solution.py:196
  357.0 5.8 multiply_reduce_fusion.5
  368.5 4.8 fusion.300
  374.4 21.8 %dynamic_update_slice.51 = f32[8,512,8,64]{1,0,3,2:T(8,128)} dynamic-update-slice(f32[8,512,8,64]{1,0,3,2:T(8,128)} %get-tuple-element.1293, f32[1,512,8,64]{1,0,3,2:T(1,128)S(1)} %copy.224, s32[]{:T(128)} %get-tuple-element.1290, s32[]{:T(128)} %constant.253.clone.1..sunk.2, s32[]{:T(128)} %constant.253.clone.1..sunk.2, s32[]{:T(128)} %constant.253.clone.1..sunk.2) | dynamic-update-slice | bytes 2097156 | tf_op jit(solution)/shard_map/while/body/jit(dynamic_update_index_in_dim)/dynamic_update_slice | solution.py:196
  417.3 5.8 multiply_reduce_fusion.5
  428.8 4.8 fusion.300
  434.7 21.8 %dynamic_update_slice.51 = f32[8,512,8,64]{1,0,3,2:T(8,128)} dynamic-update-slice(f32[8,512,8,64]{1,0,3,2:T(8,128)} %get-tuple-element.1293, f32[1,512,8,64]{1,0,3,2:T(1,128)S(1)} %copy.224, s32[]{:T(128)} %get-tuple-element.1290, s32[]{:T(128)} %constant.253.clone.1..sunk.2, s32[]{:T(128)} %constant.253.clone.1..sunk.2, s32[]{:T(128)} %constant.253.clone.1..sunk.2) | dynamic-update-slice | bytes 2097156 | tf_op jit(solution)/shard_map/while/body/jit(dynamic_update_index_in_dim)/dynamic_update_slice | solution.py:196
  477.6 5.8 multiply_reduce_fusion.5
  489.1 4.8 fusion.300
  495.0 21.8 %dynamic_update_slice.51 = f32[8,512,8,64]{1,0,3,2:T(8,128)} dynamic-update-slice(f32[8,512,8,64]{1,0,3,2:T(8,128)} %get-tuple-element.1293, f32[1,512,8,64]{1,0,3,2:T(1,128)S(1)} %copy.224, s32[]{:T(128)} %get-tuple-element.1290, s32[]{:T(128)} %constant.253.clone.1..sunk.2, s32[]{:T(128)} %constant.253.clone.1..sunk.2, s32[]{:T(128)} %constant.253.clone.1..sunk.2) | dynamic-update-slice | bytes 2097156 | tf_op jit(solution)/shard_map/while/body/jit(dynamic_update_index_in_dim)/dynamic_update_slice | solution.py:196
  538.0 5.8 multiply_reduce_fusion.5
  549.5 4.8 fusion.300
  555.3 21.8 %dynamic_update_slice.51 = f32[8,512,8,64]{1,0,3,2:T(8,128)} dynamic-update-slice(f32[8,512,8,64]{1,0,3,2:T(8,128)} %get-tuple-element.1293, f32[1,512,8,64]{1,0,3,2:T(1,128)S(1)} %copy.224, s32[]{:T(128)} %get-tuple-element.1290, s32[]{:T(128)} %constant.253.clone.1..sunk.2, s32[]{:T(128)} %constant.253.clone.1..sunk.2, s32[]{:T(128)} %constant.253.clone.1..sunk.2) | dynamic-update-slice | bytes 2097156 | tf_op jit(solution)/shard_map/while/body/jit(dynamic_update_index_in_dim)/dynamic_update_slice | solution.py:196
  584.6 10.9 all-gather
  595.5 9.1 all-gather.1
  604.6 22.9 %while.76 = (s32[]{:T(128)}, f32[8,64,64]{2,1,0:T(8,128)}, f32[8,64]{1,0:T(8,128)S(1)}, s32[]{:T(128)}, bf16[8,8,64,64]{3,2,1,0:T(8,128)(2,1)S(1)}, /*index=5*/b...) while((s32[]{:T(128)}, f32[8,64,64]{2,1,0:T(8,128)}, ...), condition=%wide.region_10.11_spmd.clone, body=%wide.region_9.10_spmd.clone.sunk | while | flops 166405 | bytes 332957 | solution.py:34
  627.6 4.8 copy.198
  632.4 9.4 reshape.432
  646.1 6.9 fusion.96
  660.8 76.4 %all-gather.11.cloned.1.call-done = bf16[4096,512]{0,1:T(8,128)(2,1)} async-done(((bf16[1024,512]{0,1:T(8,128)(2,1)}), bf16[4096,512]{0,1:T(8,128)(2,1)}) %all-gather.11.cloned.1.call-update) | async-done | bytes 4194320 | tf_op jit(solution)/shard_map/all_gather | solution.py:223
  737.2 22.8 %fusion.89 = (bf16[4096,512]{1,0:T(8,128)(2,1)}, f32[4096,512]{1,0:T(8,128)}) fusion(f32[512]{0:T(512)} %convert_element_type.335, bf16[4096,512]{0,1:T(8,128)(2,1)} %all-gather.11.cloned.1.call-done, bf16[512,512]{1,0:T(8,128)(2,1)S(1)} %copy-done), kind=kOutput, calls=%fused_computation.135 | convolution fusion | flops 2285895680 | bytes 17303552 | tf_op jit(solution)/shard_map/dot_general | solution.py:224
  760.0 58.0 %all-gather.13.cloned.1.call-done = bf16[4096,512]{1,0:T(8,128)(2,1)} async-done(((bf16[1024,512]{1,0:T(8,128)(2,1)}), bf16[4096,512]{1,0:T(8,128)(2,1)}) %all-gather.13.cloned.1.call-update) | async-done | bytes 4194320 | tf_op jit(solution)/shard_map/all_gather | solution.py:232
  818.1 8.9 convert_reduce_fusion.1
  834.3 6.6 convolution_convert_fusion.1
  840.9 10.4 all-gather.15.cloned.1.call-start
  853.7 55.1 %reduce-scatter.5.cloned.1.call-done = bf16[1024,512]{0,1:T(8,128)(2,1)} async-done(((bf16[4096,512]{0,1:T(8,128)(2,1)}), bf16[1024,512]{0,1:T(8,128)(2,1)}) %reduce-scatter.5.cloned.1.call-update) | async-done | bytes 1048592 | tf_op jit(solution)/shard_map/reduce_scatter | solution.py:242
  911.5 76.8 %reduce-scatter.3.cloned.1.call-done = bf16[1024,512]{0,1:T(8,128)(2,1)} async-done(((bf16[4096,512]{0,1:T(8,128)(2,1)}), bf16[1024,512]{0,1:T(8,128)(2,1)}) %reduce-scatter.3.cloned.1.call-update) | async-done | bytes 1048592 | tf_op jit(solution)/shard_map/reduce_scatter | solution.py:226
  998.7 5.6 fusion.156
  1011.1 66.3 %all-gather.15.cloned.1.call-done = bf16[4096,512]{1,0:T(8,128)(2,1)} async-done(((bf16[1024,512]{1,0:T(8,128)(2,1)}), bf16[4096,512]{1,0:T(8,128)(2,1)}) %all-gather.15.cloned.1.call-update) | async-done | bytes 4194320 | tf_op jit(solution)/shard_map/all_gather | solution.py:264
  1077.4 7.1 copy.158
  1084.4 7.8 multiply_reduce_fusion.1
  1092.9 5.1 fusion.139
  1098.1 8.9 all-gather.3
  1111.1 13.4 all-gather.2
  1124.5 9.7 while.73
  1134.2 5.6 broadcast_in_dim.58.clone
  1139.8 371.0 %while.74 = (s32[]{:T(128)}, f32[8,64,64]{2,1,0:T(8,128)S(1)}, f32[8,64]{1,0:T(8,128)S(1)}, bf16[8,512,1536]{2,1,0:T(8,128)(2,1)}, s32[8]{0:T(128)S(1)}, /*index...) while((s32[]{:T(128)}, f32[8,64,64]{2,1,0:T(8,128)S(1)}, ...), condition=%wide.region_21.22_spmd, body=%wide.region_20.21_spmd.sunk | while | flops 2815500288 | bytes 89005016 | solution.py:352
  1151.6 4.6 fusion.281
  1197.9 4.6 fusion.281
  1244.2 4.6 fusion.281
  1337.0 4.6 fusion.281
  1383.3 4.6 fusion.281
  1429.7 4.6 fusion.281
  1476.0 4.6 fusion.281
  1510.8 5.7 fusion.109
  1517.2 12.9 psum.77
  1531.4 5.6 fusion.153
  1546.3 38.9 %all-reduce.1 = (f32[512]{0:T(512)}, f32[512]{0:T(512)}, f32[512]{0:T(512)}, f32[512]{0:T(512)}, f32[512]{0:T(512)}) all-reduce(f32[512]{0:T(512)S(1)} %get-tuple-element.848, f32[512]{0:T(512)S(1)} %get-tuple-element.977, f32[512]{0:T(512)S(1)} %copy-done.48, f32[512]{0:T(512)S(1)} %copy-done.49, ...), channel_id=1, replica_groups=mesh['dp'=8,'mp'=4] {'dp','mp'}, use_global_device_ids=true, to_apply=%region_27.28 | all-reduce | flops 2560 | bytes 20480 | tf_op jit(solution)/shard_map/psum | solution.py:367
  1585.2 71.9 %all-reduce.7.cloned.1.call-done = (f32[512,1536]{1,0:T(8,128)}, f32[512,512]{1,0:T(8,128)}) async-done(((f32[512,1536]{1,0:T(8,128)}, f32[512,512]{1,0:T(8,128)}), (f32[512,1536]{1,0:T(8,128)}, f32[512,512]{1,0:T(8,128)})) %all-reduce.7.cloned.1.call-update) | async-done | bytes 4194320 | tf_op jit(solution)/shard_map/psum | solution.py:367
  (725 shorter events, 620.6 us)
Async XLA Ops:
  7.2 730.0 %copy-start = (bf16[512,512]{1,0:T(8,128)(2,1)S(1)}, bf16[512,512]{1,0:T(8,128)(2,1)}, u32[]{:S(2)}) copy-start(bf16[512,512]{1,0:T(8,128)(2,1)} %param.28) | copy-start | bytes 1572868
  7.2 8.6 copy-start.59
  7.2 3.1 copy-start.43
  7.2 3.1 copy-start.53
  7.2 4.6 copy-start.54
  7.2 88.1 %all-gather.9.cloned.1.call-start = ((), (), s32[]{:S(2)}) async-start(), calls=%async_computation.2 | async-start | bytes 5242880 | tf_op jit(solution)/shard_map/all_gather | solution.py:148
  8.8 93.1 %copy-start.7 = (bf16[1024,512]{0,1:T(8,128)(2,1)}, bf16[1024,512]{0,1:T(8,128)(2,1)S(1)}, u32[]{:S(2)}) copy-start(bf16[1024,512]{0,1:T(8,128)(2,1)S(1)} %copy.149) | copy-start | bytes 3145732
  11.8 725.5 %all-gather.11.cloned.1.call-start = ((), (), s32[]{:S(2)}) async-start(), calls=%async_computation.3 | async-start | bytes 5242880 | tf_op jit(solution)/shard_map/all_gather | solution.py:223
  15.2 86.6 %copy-start.28 = (f32[4096]{0:T(1024)}, f32[4096]{0:T(1024)S(1)}, u32[]{:S(2)}) copy-start(f32[4096]{0:T(1024)S(1)} %get-tuple-element.953) | copy-start | bytes 49156
  584.6 11.0 copy-start.45
  627.5 4.9 copy-start.57
  627.6 14.3 copy-start.26
  632.4 13.5 copy-start.29
  632.4 13.5 copy-start.31
  641.8 4.2 copy-start.14
  641.8 4.2 copy-start.19
  646.0 7.0 copy-start.8
  646.1 7.0 copy-start.22
  653.0 3.3 copy-start.18
  653.0 4.5 copy-start.41
  653.0 4.4 copy-start.50
  658.8 159.3 %all-gather.13.cloned.1.call-start = ((), (), s32[]{:S(2)}) async-start(), calls=%async_computation.5 | async-start | bytes 5242880 | tf_op jit(solution)/shard_map/all_gather | solution.py:232
  659.5 249.3 %reduce-scatter.5.cloned.1.call-start = ((), (), s32[]{:S(2)}) async-start(), calls=%async_computation.6 | async-start | bytes 5242880 | tf_op jit(solution)/shard_map/reduce_scatter | solution.py:242
  833.3 154.9 %reduce-scatter.3.cloned.1.call-start = ((), (), s32[]{:S(2)}) async-start(), calls=%async_computation.4 | async-start | bytes 5242880 | tf_op jit(solution)/shard_map/reduce_scatter | solution.py:226
  840.9 67.9 %copy-start.33 = (f32[1024]{0:T(1024)S(1)}, f32[1024]{0:T(1024)}, u32[]{:S(2)}) copy-start(f32[1024]{0:T(1024)} %copy-done.32) | copy-start | bytes 12292
  840.9 67.9 %copy-start.37 = (f32[1024]{0:T(1024)S(1)}, f32[1024]{0:T(1024)}, u32[]{:S(2)}) copy-start(f32[1024]{0:T(1024)} %copy-done.36) | copy-start | bytes 12292
  840.9 67.9 %copy-start.42 = (f32[512]{0:T(512)S(1)}, f32[512]{0:T(512)}, u32[]{:S(2)}) copy-start(f32[512]{0:T(512)} %param.26) | copy-start | bytes 6148
  840.9 147.3 %copy-start.51 = (f32[512]{0:T(512)S(1)}, f32[512]{0:T(512)}, u32[]{:S(2)}) copy-start(f32[512]{0:T(512)} %param.31) | copy-start | bytes 6148
  840.9 236.4 %all-gather.15.cloned.1.call-start = ((), (), s32[]{:S(2)}) async-start(), calls=%async_computation.7 | async-start | bytes 5242880 | tf_op jit(solution)/shard_map/all_gather | solution.py:264
  992.9 3.2 copy-start.30
  992.9 3.3 copy-start.27
  992.9 3.3 copy-start.40
  992.9 4.0 copy-start.21
  996.0 589.2 %all-reduce.9.cloned.1.call-start = ((), (), s32[]{:S(2)}) async-start(), calls=%async_computation.9 | async-start | bytes 4194304 | tf_op jit(solution)/shard_map/psum | solution.py:250
  998.7 5.6 copy-start.16
  998.7 5.7 copy-start.17
  1004.4 3.4 copy-start.11
  1007.7 649.3 %all-reduce.7.cloned.1.call-start = ((), (), s32[]{:S(2)}) async-start(), calls=%async_computation.8 | async-start | bytes 8388608 | tf_op jit(solution)/shard_map/psum | solution.py:367
  1084.4 22.6 %copy-start.5 = (f32[4096,512]{0,1:T(8,128)S(1)}, f32[4096,512]{0,1:T(8,128)}, u32[]{:S(2)}) copy-start(f32[4096,512]{0,1:T(8,128)} %copy.158) | copy-start | bytes 25165828
  1109.8 14.7 copy-start.58
  1150.4 5.8 copy-start.4
  1174.3 3.9 copy-start.6
  1196.7 5.8 copy-start.4
  1220.6 3.9 copy-start.6
  1243.0 5.8 copy-start.4
  1267.0 3.9 copy-start.6
  1289.4 5.8 copy-start.4
  1313.4 3.9 copy-start.6
  1335.7 5.8 copy-start.4
  1359.7 3.9 copy-start.6
  1382.1 5.8 copy-start.4
  1406.1 3.9 copy-start.6
  1428.5 5.8 copy-start.4
  1452.4 3.9 copy-start.6
  1474.8 5.8 copy-start.4
  1498.8 3.9 copy-start.6
  1516.5 13.6 copy-start.20
  1542.6 3.7 copy-start.46
  1542.6 3.7 copy-start.48
  1542.6 3.7 copy-start.49
  1657.0 3.9 copy-start.25
  1657.0 4.9 copy-start.24
  1657.0 5.9 copy-start.23
  1657.1 6.8 copy-start.1
  (33 other events, 60.1 us)
Sparse Core Ops, SparseCore 0:
  11.9 83.4 all-gather.8
  658.9 78.2 all-gather.10
  738.8 79.2 all-gather.12
  833.4 75.2 reduce-scatter.4
  910.9 77.2 reduce-scatter.2
  996.1 81.2 all-gather.14
  1080.7 61.3 all-reduce.8
  1516.7 140.3 all-reduce.6
where the time goes:
time: 1690 us; the launch traced here: 1670 us
  waiting for transfers between devices  468 us (28%)
  local copies, waits for them, and re-layouts  449 us (27%)
  matrix products  431 us (26%)
  other arithmetic  139 us (8%)
  blocking collectives  109 us (6%)
  loops' own time  48.6 us (3%)
    dynamic_update_slice x16, local copies, waits for them, and re-layouts, local(): lax.scan(forward_block, (zero_state, zero_total), jnp.arange(blocks, dtyp...  183 us
    reduce_scatter x1, waiting for transfers between devices, local(): lax.psum_scatter(jnp.dot(hidden_low, down_weight, preferred_element_type=...  76.8 us
    all_gather x1, waiting for transfers between devices, local(): group_second = lax.all_gather(second_low, 'mp', axis=0, tiled=True)  76.4 us
    psum x1, waiting for transfers between devices, local(): lax.psum((grad_qkv, grad_out, grad_gain_one, grad_shift_one, grad_gain_tw...  71.9 us
    all_gather x1, waiting for transfers between devices, local(): lax.all_gather(grad_context_own, 'mp', axis=0, tiled=True)  66.3 us
    all_gather x1, waiting for transfers between devices, local(): group_rows = lax.all_gather(normed_low, 'mp', axis=0, tiled=True)  62.3 us
    all_gather x1, waiting for transfers between devices, local(): group_cotangent = lax.all_gather(cotangent, 'mp', axis=0, tiled=True)  58 us
    reduce_scatter x1, waiting for transfers between devices, local(): lax.psum_scatter(jnp.einsum('tf,df->td', hidden_grad, up_weight, preferre...  55.1 us
  transfers between devices with their start and end apart: 8, of which 7 were waited for; matrix products, arithmetic and copies ran while one was open for 26% of the time, Pallas kernels for 0%

commit v1 on v0

--- a/solution.py
+++ b/solution.py
@@ -145,7 +145,18 @@
     inputs = tokens.astype(jnp.float32)
     normed_one, scaled_one, inv_one = normalize(inputs, norm1_gain, norm1_shift)
     normed_low = normed_one.astype(jnp.bfloat16)
-    group_rows = lax.all_gather(normed_low, "mp", axis=0, tiled=True)
+    n_blocks = lax.psum(1, axis_name="mp")
+    block_list = [normed_low]
+    for d in range(1, n_blocks):
+        block_list.append(
+            lax.ppermute(
+                block_list[d - 1],
+                axis_name="mp",
+                perm=[(tick, (tick - 1) % n_blocks) for tick in range(n_blocks)],
+            )
+        )
+    b_next = jnp.concatenate(block_list, axis=0)
+    group_rows = jnp.roll(b_next, shift=lax.axis_index("mp") * normed_low.shape[0], axis=0)
 
     def features(start):
         rows_in = lax.dynamic_slice_in_dim(group_rows, start, BLK)

time: 1690 us -> 1700 us (level)
  local copies, waits for them, and re-layouts: 449 us -> 468 us
    all_gather x1 -> x0, waiting for transfers between devices: 62.3 us -> none  [local(): group_rows = lax.all_gather(normed_low, 'mp', axis=0, tiled=True)]
    ppermute x0 -> x3, waiting for transfers between devices: none -> 44 us  [local(): lax.ppermute(block_list[d - 1], axis_name='mp', perm=[(tick, (tick - 1) %...]
    unnamed x126 -> x138, local copies, waits for them, and re-layouts: 33.2 us -> 44.7 us
  transfers between devices with their start and end apart: 8 -> 10, of which waited for: 7 -> 8; matrix products, arithmetic and copies ran while one was open for 26% -> 27% of each run, Pallas kernels for 0% -> 0%
where the time goes in v1:
time: 1700 us; the launch traced here: 1680 us
  local copies, waits for them, and re-layouts  468 us (28%)
  waiting for transfers between devices  462 us (27%)
  matrix products  431 us (25%)
  other arithmetic  139 us (8%)
  blocking collectives  105 us (6%)
  loops' own time  48.6 us (3%)
    dynamic_update_slice x16, local copies, waits for them, and re-layouts, local(): lax.scan(forward_block, (zero_state, zero_total), jnp.arange(blocks, dtyp...  183 us
    all_gather x1, waiting for transfers between devices, local(): group_second = lax.all_gather(second_low, 'mp', axis=0, tiled=True)  78.9 us
    reduce_scatter x1, waiting for transfers between devices, local(): lax.psum_scatter(jnp.dot(hidden_low, down_weight, preferred_element_type=...  76.8 us
    psum x1, waiting for transfers between devices, local(): lax.psum((grad_qkv, grad_out, grad_gain_one, grad_shift_one, grad_gain_tw...  71.6 us
    all_gather x1, waiting for transfers between devices, local(): lax.all_gather(grad_context_own, 'mp', axis=0, tiled=True)  66.3 us
    reduce_scatter x1, waiting for transfers between devices, local(): lax.psum_scatter(jnp.einsum('tf,df->td', hidden_grad, up_weight, preferre...  65.3 us
    all_gather x1, waiting for transfers between devices, local(): group_cotangent = lax.all_gather(cotangent, 'mp', axis=0, tiled=True)  58.1 us
    dot_general x8, matrix products, forward_block(): jnp.einsum('ihd,jhd->hij', query_low, key_low, preferred_element_type=jnp...  46.3 us
  transfers between devices with their start and end apart: 10, of which 8 were waited for; matrix products, arithmetic and copies ran while one was open for 27% of the time, Pallas kernels for 0%

profile of v1, /device:TPU:0, one launch (start us, length us, event | category | flops | bytes accessed | tf_op | source)
XLA Modules:
  0.0 1684.2 jit_solution(15356356037390488397)
XLA Ops:
  10.8 5.1 collective-permute-start
  15.9 22.4 %collective-permute-done = bf16[1024,512]{0,1:T(8,128)(2,1)S(1)} collective-permute-done((bf16[1024,512]{0,1:T(8,128)(2,1)S(1)}, bf16[1024,512]{0,1:T(8,128)(2,1)S(1)}, u32[]{:S(2)}, u32[]{:S(2)}) %collective-permute-start) | collective-permute-done | bytes 1048608 | tf_op jit(solution)/shard_map/ppermute | solution.py:152
  43.6 21.6 %collective-permute-done.1 = bf16[1024,512]{0,1:T(8,128)(2,1)} collective-permute-done((bf16[1024,512]{0,1:T(8,128)(2,1)S(1)}, bf16[1024,512]{0,1:T(8,128)(2,1)}, u32[]{:S(2)}, u32[]{:S(2)}) %collective-permute-start.1) | collective-permute-done | bytes 1048608 | tf_op jit(solution)/shard_map/ppermute | solution.py:152
  75.5 12.0 all-reduce
  101.4 4.7 constant_dynamic-slice_fusion.1
  106.1 6.5 copy.151
  112.7 483.1 %while.75 = (s32[]{:T(128)}, f32[8,64,64]{2,1,0:T(8,128)S(1)}, f32[8,64]{1,0:T(8,128)S(1)}, f32[8,512,8,64]{1,0,3,2:T(8,128)}, f32[8,512,8]{1,2,0:T(8,128)}, /*i...) while((s32[]{:T(128)}, f32[8,64,64]{2,1,0:T(8,128)S(1)}, ...), condition=%wide.region_8.9_spmd.clone, body=%wide.region_5.8_spmd.clone.sunk | while | flops 1599254528 | bytes 64349520 | solution.py:207
  126.4 5.8 multiply_reduce_fusion.5
  137.9 4.8 fusion.301
  143.8 21.8 %dynamic_update_slice.51 = f32[8,512,8,64]{1,0,3,2:T(8,128)} dynamic-update-slice(f32[8,512,8,64]{1,0,3,2:T(8,128)} %get-tuple-element.1295, f32[1,512,8,64]{1,0,3,2:T(1,128)S(1)} %copy.224, s32[]{:T(128)} %get-tuple-element.1292, s32[]{:T(128)} %constant.271.clone.1..sunk.2, s32[]{:T(128)} %constant.271.clone.1..sunk.2, s32[]{:T(128)} %constant.271.clone.1..sunk.2) | dynamic-update-slice | bytes 2097156 | tf_op jit(solution)/shard_map/while/body/jit(dynamic_update_index_in_dim)/dynamic_update_slice | solution.py:207
  186.8 5.8 multiply_reduce_fusion.5
  198.4 4.8 fusion.301
  204.2 21.8 %dynamic_update_slice.51 = f32[8,512,8,64]{1,0,3,2:T(8,128)} dynamic-update-slice(f32[8,512,8,64]{1,0,3,2:T(8,128)} %get-tuple-element.1295, f32[1,512,8,64]{1,0,3,2:T(1,128)S(1)} %copy.224, s32[]{:T(128)} %get-tuple-element.1292, s32[]{:T(128)} %constant.271.clone.1..sunk.2, s32[]{:T(128)} %constant.271.clone.1..sunk.2, s32[]{:T(128)} %constant.271.clone.1..sunk.2) | dynamic-update-slice | bytes 2097156 | tf_op jit(solution)/shard_map/while/body/jit(dynamic_update_index_in_dim)/dynamic_update_slice | solution.py:207
  247.2 5.8 multiply_reduce_fusion.5
  258.7 4.8 fusion.301
  264.6 21.8 %dynamic_update_slice.51 = f32[8,512,8,64]{1,0,3,2:T(8,128)} dynamic-update-slice(f32[8,512,8,64]{1,0,3,2:T(8,128)} %get-tuple-element.1295, f32[1,512,8,64]{1,0,3,2:T(1,128)S(1)} %copy.224, s32[]{:T(128)} %get-tuple-element.1292, s32[]{:T(128)} %constant.271.clone.1..sunk.2, s32[]{:T(128)} %constant.271.clone.1..sunk.2, s32[]{:T(128)} %constant.271.clone.1..sunk.2) | dynamic-update-slice | bytes 2097156 | tf_op jit(solution)/shard_map/while/body/jit(dynamic_update_index_in_dim)/dynamic_update_slice | solution.py:207
  307.6 5.8 multiply_reduce_fusion.5
  319.1 4.8 fusion.301
  325.0 21.8 %dynamic_update_slice.51 = f32[8,512,8,64]{1,0,3,2:T(8,128)} dynamic-update-slice(f32[8,512,8,64]{1,0,3,2:T(8,128)} %get-tuple-element.1295, f32[1,512,8,64]{1,0,3,2:T(1,128)S(1)} %copy.224, s32[]{:T(128)} %get-tuple-element.1292, s32[]{:T(128)} %constant.271.clone.1..sunk.2, s32[]{:T(128)} %constant.271.clone.1..sunk.2, s32[]{:T(128)} %constant.271.clone.1..sunk.2) | dynamic-update-slice | bytes 2097156 | tf_op jit(solution)/shard_map/while/body/jit(dynamic_update_index_in_dim)/dynamic_update_slice | solution.py:207
  368.0 5.8 multiply_reduce_fusion.5
  379.5 4.8 fusion.301
  385.4 21.8 %dynamic_update_slice.51 = f32[8,512,8,64]{1,0,3,2:T(8,128)} dynamic-update-slice(f32[8,512,8,64]{1,0,3,2:T(8,128)} %get-tuple-element.1295, f32[1,512,8,64]{1,0,3,2:T(1,128)S(1)} %copy.224, s32[]{:T(128)} %get-tuple-element.1292, s32[]{:T(128)} %constant.271.clone.1..sunk.2, s32[]{:T(128)} %constant.271.clone.1..sunk.2, s32[]{:T(128)} %constant.271.clone.1..sunk.2) | dynamic-update-slice | bytes 2097156 | tf_op jit(solution)/shard_map/while/body/jit(dynamic_update_index_in_dim)/dynamic_update_slice | solution.py:207
  428.4 5.8 multiply_reduce_fusion.5
  439.9 4.8 fusion.301
  445.7 21.8 %dynamic_update_slice.51 = f32[8,512,8,64]{1,0,3,2:T(8,128)} dynamic-update-slice(f32[8,512,8,64]{1,0,3,2:T(8,128)} %get-tuple-element.1295, f32[1,512,8,64]{1,0,3,2:T(1,128)S(1)} %copy.224, s32[]{:T(128)} %get-tuple-element.1292, s32[]{:T(128)} %constant.271.clone.1..sunk.2, s32[]{:T(128)} %constant.271.clone.1..sunk.2, s32[]{:T(128)} %constant.271.clone.1..sunk.2) | dynamic-update-slice | bytes 2097156 | tf_op jit(solution)/shard_map/while/body/jit(dynamic_update_index_in_dim)/dynamic_update_slice | solution.py:207
  488.7 5.8 multiply_reduce_fusion.5
  500.2 4.8 fusion.301
  506.1 21.8 %dynamic_update_slice.51 = f32[8,512,8,64]{1,0,3,2:T(8,128)} dynamic-update-slice(f32[8,512,8,64]{1,0,3,2:T(8,128)} %get-tuple-element.1295, f32[1,512,8,64]{1,0,3,2:T(1,128)S(1)} %copy.224, s32[]{:T(128)} %get-tuple-element.1292, s32[]{:T(128)} %constant.271.clone.1..sunk.2, s32[]{:T(128)} %constant.271.clone.1..sunk.2, s32[]{:T(128)} %constant.271.clone.1..sunk.2) | dynamic-update-slice | bytes 2097156 | tf_op jit(solution)/shard_map/while/body/jit(dynamic_update_index_in_dim)/dynamic_update_slice | solution.py:207
  549.1 5.8 multiply_reduce_fusion.5
  560.6 4.8 fusion.301
  566.5 21.8 %dynamic_update_slice.51 = f32[8,512,8,64]{1,0,3,2:T(8,128)} dynamic-update-slice(f32[8,512,8,64]{1,0,3,2:T(8,128)} %get-tuple-element.1295, f32[1,512,8,64]{1,0,3,2:T(1,128)S(1)} %copy.224, s32[]{:T(128)} %get-tuple-element.1292, s32[]{:T(128)} %constant.271.clone.1..sunk.2, s32[]{:T(128)} %constant.271.clone.1..sunk.2, s32[]{:T(128)} %constant.271.clone.1..sunk.2) | dynamic-update-slice | bytes 2097156 | tf_op jit(solution)/shard_map/while/body/jit(dynamic_update_index_in_dim)/dynamic_update_slice | solution.py:207
  595.8 11.0 all-gather
  606.7 8.4 all-gather.1
  615.2 22.9 %while.76 = (s32[]{:T(128)}, f32[8,64,64]{2,1,0:T(8,128)}, f32[8,64]{1,0:T(8,128)S(1)}, s32[]{:T(128)}, bf16[8,8,64,64]{3,2,1,0:T(8,128)(2,1)S(1)}, /*index=5*/b...) while((s32[]{:T(128)}, f32[8,64,64]{2,1,0:T(8,128)}, ...), condition=%wide.region_10.11_spmd.clone, body=%wide.region_9.10_spmd.clone.sunk | while | flops 166405 | bytes 332957 | solution.py:34
  638.1 4.8 copy.198
  642.9 9.4 reshape.432
  656.6 6.9 fusion.96
  671.3 78.9 %all-gather.8.cloned.1.call-done = bf16[4096,512]{0,1:T(8,128)(2,1)} async-done(((bf16[1024,512]{0,1:T(8,128)(2,1)}), bf16[4096,512]{0,1:T(8,128)(2,1)}) %all-gather.8.cloned.1.call-update) | async-done | bytes 4194320 | tf_op jit(solution)/shard_map/all_gather | solution.py:234
  750.2 22.8 %fusion.89 = (bf16[4096,512]{1,0:T(8,128)(2,1)}, f32[4096,512]{1,0:T(8,128)}) fusion(f32[512]{0:T(512)} %convert_element_type.335, bf16[4096,512]{0,1:T(8,128)(2,1)} %all-gather.8.cloned.1.call-done, bf16[512,512]{1,0:T(8,128)(2,1)S(1)} %copy-done), kind=kOutput, calls=%fused_computation.135 | convolution fusion | flops 2285895680 | bytes 17303552 | tf_op jit(solution)/shard_map/dot_general | solution.py:235
  773.0 58.1 %all-gather.10.cloned.1.call-done = bf16[4096,512]{1,0:T(8,128)(2,1)} async-done(((bf16[1024,512]{1,0:T(8,128)(2,1)}), bf16[4096,512]{1,0:T(8,128)(2,1)}) %all-gather.10.cloned.1.call-update) | async-done | bytes 4194320 | tf_op jit(solution)/shard_map/all_gather | solution.py:243
  831.0 8.9 convert_reduce_fusion.1
  847.3 6.6 convolution_convert_fusion.1
  856.4 65.3 %reduce-scatter.5.cloned.1.call-done = bf16[1024,512]{0,1:T(8,128)(2,1)} async-done(((bf16[4096,512]{0,1:T(8,128)(2,1)}), bf16[1024,512]{0,1:T(8,128)(2,1)}) %reduce-scatter.5.cloned.1.call-update) | async-done | bytes 1048592 | tf_op jit(solution)/shard_map/reduce_scatter | solution.py:253
  924.4 76.8 %reduce-scatter.3.cloned.1.call-done = bf16[1024,512]{0,1:T(8,128)(2,1)} async-done(((bf16[4096,512]{0,1:T(8,128)(2,1)}), bf16[1024,512]{0,1:T(8,128)(2,1)}) %reduce-scatter.3.cloned.1.call-update) | async-done | bytes 1048592 | tf_op jit(solution)/shard_map/reduce_scatter | solution.py:237
  1011.7 5.6 fusion.157
  1024.1 66.3 %all-gather.12.cloned.1.call-done = bf16[4096,512]{1,0:T(8,128)(2,1)} async-done(((bf16[1024,512]{1,0:T(8,128)(2,1)}), bf16[4096,512]{1,0:T(8,128)(2,1)}) %all-gather.12.cloned.1.call-update) | async-done | bytes 4194320 | tf_op jit(solution)/shard_map/all_gather | solution.py:275
  1090.4 7.0 copy.158
  1097.4 7.8 multiply_reduce_fusion.1
  1105.9 5.1 fusion.139
  1111.0 8.9 all-gather.3
  1124.0 13.2 all-gather.2
  1137.2 9.7 while.73
  1147.0 5.6 broadcast_in_dim.58.clone
  1152.6 371.5 %while.74 = (s32[]{:T(128)}, f32[8,64,64]{2,1,0:T(8,128)S(1)}, f32[8,64]{1,0:T(8,128)S(1)}, bf16[8,512,1536]{2,1,0:T(8,128)(2,1)}, s32[8]{0:T(128)S(1)}, /*index...) while((s32[]{:T(128)}, f32[8,64,64]{2,1,0:T(8,128)S(1)}, ...), condition=%wide.region_21.22_spmd, body=%wide.region_20.21_spmd.sunk | while | flops 2815500288 | bytes 89005016 | solution.py:363
  1164.4 4.6 fusion.282
  1210.8 4.6 fusion.282
  1257.2 4.6 fusion.282
  1350.1 4.6 fusion.282
  1396.5 4.6 fusion.282
  1524.0 5.7 fusion.109
  1530.4 12.9 psum.77
  1544.6 5.6 fusion.154
  1559.6 39.1 %all-reduce.1 = (f32[512]{0:T(512)}, f32[512]{0:T(512)}, f32[512]{0:T(512)}, f32[512]{0:T(512)}, f32[512]{0:T(512)}) all-reduce(f32[512]{0:T(512)S(1)} %get-tuple-element.848, f32[512]{0:T(512)S(1)} %get-tuple-element.979, f32[512]{0:T(512)S(1)} %copy-done.51, f32[512]{0:T(512)S(1)} %copy-done.52, ...), channel_id=1, replica_groups=mesh['dp'=8,'mp'=4] {'dp','mp'}, use_global_device_ids=true, to_apply=%region_27.28 | all-reduce | flops 2560 | bytes 20480 | tf_op jit(solution)/shard_map/psum | solution.py:378
  1598.7 71.6 %all-reduce.7.cloned.1.call-done = (f32[512,1536]{1,0:T(8,128)}, f32[512,512]{1,0:T(8,128)}) async-done(((f32[512,1536]{1,0:T(8,128)}, f32[512,512]{1,0:T(8,128)}), (f32[512,1536]{1,0:T(8,128)}, f32[512,512]{1,0:T(8,128)})) %all-reduce.7.cloned.1.call-update) | async-done | bytes 4194320 | tf_op jit(solution)/shard_map/psum | solution.py:378
  (742 shorter events, 653.0 us)
Async XLA Ops:
  7.2 743.0 %copy-start = (bf16[512,512]{1,0:T(8,128)(2,1)S(1)}, bf16[512,512]{1,0:T(8,128)(2,1)}, u32[]{:S(2)}) copy-start(bf16[512,512]{1,0:T(8,128)(2,1)} %param.28) | copy-start | bytes 1572868
  7.2 66.3 %copy-start.62 = (u32[32]{0:T(128)S(1)}, u32[32]{0:T(128)}, u32[]{:S(2)}) copy-start(u32[32]{0:T(128)} %constant.319) | copy-start | bytes 388
  7.2 62.3 %copy-start.57 = (s32[17]{0:T(128)S(1)}, s32[17]{0:T(128)}, u32[]{:S(2)}) copy-start(s32[17]{0:T(128)} %param.32) | copy-start | bytes 208
  7.2 743.0 %all-gather.8.cloned.1.call-start = ((), (), s32[]{:S(2)}) async-start(), calls=%async_computation.2 | async-start | bytes 5242880 | tf_op jit(solution)/shard_map/all_gather | solution.py:234
  8.8 83.5 %copy-start.7 = (bf16[1024,512]{0,1:T(8,128)(2,1)}, bf16[1024,512]{0,1:T(8,128)(2,1)S(1)}, u32[]{:S(2)}) copy-start(bf16[1024,512]{0,1:T(8,128)(2,1)S(1)} %copy.149) | copy-start | bytes 3145732
  9.0 56.1 %copy-start.37 = (f32[1024]{0:T(1024)}, f32[1024]{0:T(1024)S(1)}, u32[]{:S(2)}) copy-start(f32[1024]{0:T(1024)S(1)} %broadcast_multiply_fusion.5) | copy-start | bytes 12292
  9.4 60.1 %copy-start.41 = (f32[1024]{0:T(1024)}, f32[1024]{0:T(1024)S(1)}, u32[]{:S(2)}) copy-start(f32[1024]{0:T(1024)S(1)} %add_rsqrt_fusion.1) | copy-start | bytes 12292
  10.8 84.9 %copy-start.21 = (bf16[1024,512]{0,1:T(8,128)(2,1)}, bf16[1024,512]{0,1:T(8,128)(2,1)S(1)}, u32[]{:S(2)}) copy-start(bf16[1024,512]{0,1:T(8,128)(2,1)S(1)} %get-tuple-element.955) | copy-start | bytes 3145732
  10.8 27.5 %collective-permute-start = (bf16[1024,512]{0,1:T(8,128)(2,1)S(1)}, bf16[1024,512]{0,1:T(8,128)(2,1)S(1)}, u32[]{:S(2)}, u32[]{:S(2)}) collective-permute-start(bf16[1024,512]{0,1:T(8,128)(2,1)S(1)} %get-tuple-element.955), channel_id=1, source_target_pairs={{0,3},{1,0},{2,1},{3,2},{4,7},{5,4},{6,5},{7,6},{8,11},{9,8},{10,9... | collective-permute-start | bytes 3145736 | tf_op jit(solution)/shard_map/ppermute | solution.py:152
  39.3 25.8 %collective-permute-start.1 = (bf16[1024,512]{0,1:T(8,128)(2,1)S(1)}, bf16[1024,512]{0,1:T(8,128)(2,1)}, u32[]{:S(2)}, u32[]{:S(2)}) collective-permute-start(bf16[1024,512]{0,1:T(8,128)(2,1)S(1)} %collective-permute-done), channel_id=1, source_target_pairs={{0,3},{1,0},{2,1},{3,2},{4,7},{5,4},{6,5},{7,6},{8,11},{9,8},{10,9... | collective-permute-start | bytes 3145736 | tf_op jit(solution)/shard_map/ppermute | solution.py:152
  65.1 27.1 %collective-permute-start.2 = (bf16[1024,512]{0,1:T(8,128)(2,1)}, bf16[1024,512]{0,1:T(8,128)(2,1)}, u32[]{:S(2)}, u32[]{:S(2)}) collective-permute-start(bf16[1024,512]{0,1:T(8,128)(2,1)} %collective-permute-done.1), channel_id=1, source_target_pairs={{0,3},{1,0},{2,1},{3,2},{4,7},{5,4},{6,5},{7,6},{8,11},{9,8},{10,9... | collective-permute-start | bytes 3145736 | tf_op jit(solution)/shard_map/ppermute | solution.py:152
  72.9 22.8 %copy-start.31 = (f32[4096]{0:T(1024)}, f32[4096]{0:T(1024)S(1)}, u32[]{:S(2)}) copy-start(f32[4096]{0:T(1024)S(1)} %get-tuple-element.953) | copy-start | bytes 49156
  87.6 8.2 copy-start.23
  595.7 11.0 copy-start.48
  638.1 4.9 copy-start.60
  638.1 14.3 copy-start.29
  642.9 13.5 copy-start.32
  642.9 13.5 copy-start.34
  652.3 4.2 copy-start.14
  652.3 4.2 copy-start.19
  656.5 7.0 copy-start.8
  656.6 7.0 copy-start.25
  663.5 4.4 copy-start.46
  663.5 4.4 copy-start.54
  669.3 161.8 %all-gather.10.cloned.1.call-start = ((), (), s32[]{:S(2)}) async-start(), calls=%async_computation.4 | async-start | bytes 5242880 | tf_op jit(solution)/shard_map/all_gather | solution.py:243
  670.0 251.7 %reduce-scatter.5.cloned.1.call-start = ((), (), s32[]{:S(2)}) async-start(), calls=%async_computation.5 | async-start | bytes 5242880 | tf_op jit(solution)/shard_map/reduce_scatter | solution.py:253
  846.3 154.9 %reduce-scatter.3.cloned.1.call-start = ((), (), s32[]{:S(2)}) async-start(), calls=%async_computation.3 | async-start | bytes 5242880 | tf_op jit(solution)/shard_map/reduce_scatter | solution.py:237
  853.9 67.9 %copy-start.36 = (f32[1024]{0:T(1024)S(1)}, f32[1024]{0:T(1024)}, u32[]{:S(2)}) copy-start(f32[1024]{0:T(1024)} %copy-done.35) | copy-start | bytes 12292
  853.9 67.9 %copy-start.40 = (f32[1024]{0:T(1024)S(1)}, f32[1024]{0:T(1024)}, u32[]{:S(2)}) copy-start(f32[1024]{0:T(1024)} %copy-done.39) | copy-start | bytes 12292
  853.9 67.9 %copy-start.47 = (f32[512]{0:T(512)S(1)}, f32[512]{0:T(512)}, u32[]{:S(2)}) copy-start(f32[512]{0:T(512)} %param.26) | copy-start | bytes 6148
  853.9 147.3 %copy-start.55 = (f32[512]{0:T(512)S(1)}, f32[512]{0:T(512)}, u32[]{:S(2)}) copy-start(f32[512]{0:T(512)} %param.31) | copy-start | bytes 6148
  853.9 236.5 %all-gather.12.cloned.1.call-start = ((), (), s32[]{:S(2)}) async-start(), calls=%async_computation.6 | async-start | bytes 5242880 | tf_op jit(solution)/shard_map/all_gather | solution.py:275
  1005.9 4.0 copy-start.24
  1009.0 589.7 %all-reduce.9.cloned.1.call-start = ((), (), s32[]{:S(2)}) async-start(), calls=%async_computation.8 | async-start | bytes 4194304 | tf_op jit(solution)/shard_map/psum | solution.py:261
  1011.7 5.7 copy-start.16
  1011.7 5.7 copy-start.17
  1017.4 3.4 copy-start.11
  1020.7 649.5 %all-reduce.7.cloned.1.call-start = ((), (), s32[]{:S(2)}) async-start(), calls=%async_computation.7 | async-start | bytes 8388608 | tf_op jit(solution)/shard_map/psum | solution.py:378
  1097.4 22.5 %copy-start.5 = (f32[4096,512]{0,1:T(8,128)S(1)}, f32[4096,512]{0,1:T(8,128)}, u32[]{:S(2)}) copy-start(f32[4096,512]{0,1:T(8,128)} %copy.158) | copy-start | bytes 25165828
  1122.8 14.5 copy-start.61
  1163.2 5.8 copy-start.4
  1187.1 3.9 copy-start.6
  1209.6 5.8 copy-start.4
  1233.5 3.9 copy-start.6
  1256.0 5.8 copy-start.4
  1279.9 3.9 copy-start.6
  1302.5 5.8 copy-start.4
  1326.4 3.9 copy-start.6
  1348.9 5.8 copy-start.4
  1372.8 3.9 copy-start.6
  1395.3 5.8 copy-start.4
  1419.2 3.9 copy-start.6
  1441.7 5.8 copy-start.4
  1465.6 3.9 copy-start.6
  1488.1 5.8 copy-start.4
  1512.0 3.9 copy-start.6
  1529.7 13.6 copy-start.20
  1555.8 3.7 copy-start.49
  1555.8 3.7 copy-start.51
  1555.9 3.7 copy-start.52
  1670.3 3.9 copy-start.28
  1670.3 4.9 copy-start.27
  1670.3 5.9 copy-start.26
  1670.3 6.8 copy-start.1
  (38 other events, 77.2 us)
Sparse Core Ops, SparseCore 0:
  669.4 80.7 all-gather.7
  751.8 79.2 all-gather.9
  846.4 75.2 reduce-scatter.4
  923.9 77.2 reduce-scatter.2
  1009.1 81.2 all-gather.11
  1093.5 61.3 all-reduce.8
  1529.9 140.3 all-reduce.6
